TPU v7x, 128 devices: a whole 4x4x4 slice. The times are simulated.
128 devices in a mesh: tiles: 16 (over y, x), gauss: 8 (over z, core).
Axes of the slice: x: 4, y: 4, z: 4, core: 2. Of those that a mesh axis runs over, the one named last changes fastest.
Arguments:
- params: float32 [59, 2097152], P(None, ('tiles', 'gauss')), may hold values from -9 to 4.5, as said below
- adam_m: float32 [59, 2097152], P(None, ('tiles', 'gauss')), may hold values from -0.03 to 0.03
- adam_v: float32 [59, 2097152], P(None, ('tiles', 'gauss')), may hold values from 0.05 to 2
- cameras: float32 [4, 13], replicated, may hold values from -0.5 to 2000, as said below
- exposure: float32 [4, 3], replicated, may hold values from 0.5 to 1.5
- entry_owner: int32 [512, 1024], P(('tiles', 'gauss')), may hold values from 0 to 127, as said below
- entry_local: int32 [512, 1024], P(('tiles', 'gauss')), may hold values from 0 to 16383
- block_counts: int32 [512], P(('tiles', 'gauss')), may hold values from 2 to 4, as said below
- tile_view: int32 [512], P(('tiles', 'gauss')), may hold values from 0 to 3
- tile_spot: int32 [512], P(('tiles', 'gauss')), may hold values from 12580 to 19579
- d_image: float32 [512, 3, 256], P(('tiles', 'gauss')), may hold values from -320 to 320
Outputs:
- new_params: float32 [59, 2097152], P(None, ('tiles', 'gauss'))
- new_m: float32 [59, 2097152], P(None, ('tiles', 'gauss'))
- new_v: float32 [59, 2097152], P(None, ('tiles', 'gauss'))
- exposure_grad: float32 [4, 3], replicated
Inputs may be any that keep to these rules, and one draw needn't show every extreme that they name: `params`: components 0 to 2 lie in -4.5 to 4.5, components 3 to 5 in -5 to -2, component 6 in 0.5 to 1.5, component 10 in -9 to -7.5. `cameras`: each row holds a matrix whose entries differ from the identity's by at most 0.1, a translation with first two entries in -0.5 to 0.5 and third in 5 to 6, and a focal length in 1400 to 2000. `entry_owner`: of the 4096 entries of one device's lists (rendered or not), at most 48 name any one owner; in every draw one owner is named exactly 48 times by every device. `block_counts`: every device holds a tile of 4 blocks.
All inputs are finite; a program needn't handle non-finite values.
Results may differ from a plain program's by a relative error of at most 0.0003.
Values sent between devices are 32-bit elements; how exact they have to be, the bound alone decides.
No kernel may reach another device: no remote copies, remote signals or barrier semaphores. Data moves between devices by JAX's collectives and lax.ppermute only.
A program may use at most 256 MiB of HBM per device.

v0:
```python
import jax
import jax.numpy as jnp
from jax import lax
from jax.sharding import PartitionSpec as P

VIEWS = 4
BLOCK = 256
TILE = 16
IMG_W = 3840
IMG_H = 2160
PARAMS = 59
TPIX = 256
sh_c0 = 0.28209479177387814
sh_c1 = 0.4886025119029199
sh_c2 = (
    1.0925484305920792,
    -1.0925484305920792,
    0.31539156525252005,
    -1.0925484305920792,
    0.5462742152960396,
)
sh_c3 = (
    -0.5900435899266435,
    2.890611442640554,
    -0.4570457994644658,
    0.3731763325901154,
    -0.4570457994644658,
    1.445305721320277,
    -0.5900435899266435,
)
beta_first = 0.9
beta_second = 0.999
learn_rate = 0.01
adam_eps = 1e-08
fix_first = 1.0
fix_second = 0.632304575229036
blur_add = 0.3


def sh_color(values, unit_x, unit_y, unit_z):
    coefficients = [values[11 + 3 * index_k : 14 + 3 * index_k] for index_k in range(16)]
    square_x = unit_x * unit_x
    square_y = unit_y * unit_y
    square_z = unit_z * unit_z
    basis_list = [
        -sh_c1 * unit_y,
        sh_c1 * unit_z,
        -sh_c1 * unit_x,
        sh_c2[0] * unit_x * unit_y,
        sh_c2[1] * unit_y * unit_z,
        sh_c2[2] * (2.0 * square_z - square_x - square_y),
        sh_c2[3] * unit_x * unit_z,
        sh_c2[4] * (square_x - square_y),
        sh_c3[0] * unit_y * (3.0 * square_x - square_y),
        sh_c3[1] * unit_x * unit_y * unit_z,
        sh_c3[2] * unit_y * (4.0 * square_z - square_x - square_y),
        sh_c3[3] * unit_z * (2.0 * square_z - 3.0 * square_x - 3.0 * square_y),
        sh_c3[4] * unit_x * (4.0 * square_z - square_x - square_y),
        sh_c3[5] * unit_z * (square_x - square_y),
        sh_c3[6] * unit_x * (square_x - 3.0 * square_y),
    ]
    summed = 0.5 + sh_c0 * coefficients[0]
    for index_k in range(15):
        summed = summed + basis_list[index_k] * coefficients[index_k + 1]
    return jnp.maximum(summed, 0.0)


def project(values, camera):
    points = [values[0], values[1], values[2]]
    matrix = [[camera[3 * row_at + col_at] for col_at in range(3)] for row_at in range(3)]
    translation = [camera[9], camera[10], camera[11]]
    focal_len = camera[12]
    viewed = [
        matrix[row_at][0] * points[0]
        + matrix[row_at][1] * points[1]
        + matrix[row_at][2] * points[2]
        + translation[row_at]
        for row_at in range(3)
    ]
    inverse_depth = 1.0 / viewed[2]
    screen_x = focal_len * viewed[0] * inverse_depth + 0.5 * IMG_W
    screen_y = focal_len * viewed[1] * inverse_depth + 0.5 * IMG_H
    slope_x = focal_len * viewed[0] * inverse_depth * inverse_depth
    slope_y = focal_len * viewed[1] * inverse_depth * inverse_depth
    jac_w = [
        [
            focal_len * inverse_depth * matrix[0][col_at] - slope_x * matrix[2][col_at]
            for col_at in range(3)
        ],
        [
            focal_len * inverse_depth * matrix[1][col_at] - slope_y * matrix[2][col_at]
            for col_at in range(3)
        ],
    ]
    quat_len = jnp.sqrt(
        values[6] * values[6]
        + values[7] * values[7]
        + values[8] * values[8]
        + values[9] * values[9]
    )
    quat_w = values[6] / quat_len
    quat_x = values[7] / quat_len
    quat_y = values[8] / quat_len
    quat_z = values[9] / quat_len
    rotation = [
        [
            1.0 - 2.0 * (quat_y * quat_y + quat_z * quat_z),
            2.0 * (quat_x * quat_y - quat_w * quat_z),
            2.0 * (quat_x * quat_z + quat_w * quat_y),
        ],
        [
            2.0 * (quat_x * quat_y + quat_w * quat_z),
            1.0 - 2.0 * (quat_x * quat_x + quat_z * quat_z),
            2.0 * (quat_y * quat_z - quat_w * quat_x),
        ],
        [
            2.0 * (quat_x * quat_z - quat_w * quat_y),
            2.0 * (quat_y * quat_z + quat_w * quat_x),
            1.0 - 2.0 * (quat_x * quat_x + quat_y * quat_y),
        ],
    ]
    extent = [jnp.exp(values[3]), jnp.exp(values[4]), jnp.exp(values[5])]
    spread = [
        [
            (
                jac_w[row_at][0] * rotation[0][col_at]
                + jac_w[row_at][1] * rotation[1][col_at]
                + jac_w[row_at][2] * rotation[2][col_at]
            )
            * extent[col_at]
            for col_at in range(3)
        ]
        for row_at in range(2)
    ]
    cov_a = (
        spread[0][0] * spread[0][0]
        + spread[0][1] * spread[0][1]
        + spread[0][2] * spread[0][2]
        + blur_add
    )
    cov_b = spread[0][0] * spread[1][0] + spread[0][1] * spread[1][1] + spread[0][2] * spread[1][2]
    cov_c = (
        spread[1][0] * spread[1][0]
        + spread[1][1] * spread[1][1]
        + spread[1][2] * spread[1][2]
        + blur_add
    )
    determinant = cov_a * cov_c - cov_b * cov_b
    opacity = jax.nn.sigmoid(values[10])
    center = [
        -(
            matrix[0][col_at] * translation[0]
            + matrix[1][col_at] * translation[1]
            + matrix[2][col_at] * translation[2]
        )
        for col_at in range(3)
    ]
    offset = [points[col_at] - center[col_at] for col_at in range(3)]
    distance = jnp.sqrt(offset[0] * offset[0] + offset[1] * offset[1] + offset[2] * offset[2])
    colors = sh_color(values, offset[0] / distance, offset[1] / distance, offset[2] / distance)
    first_rows = jnp.stack(
        [
            screen_x,
            screen_y,
            cov_c / determinant,
            -cov_b / determinant,
            cov_a / determinant,
            opacity,
        ]
    )
    return jnp.concatenate([first_rows, colors], axis=0)


def render_blocks(proj_rows, live_mask, pix_x, pix_y):
    nblocks = proj_rows.shape[1] // BLOCK
    grouped = proj_rows.reshape(proj_rows.shape[0], nblocks, BLOCK).transpose(1, 0, 2)
    block_masks = live_mask.reshape(nblocks, BLOCK)

    def block_step(carried, block_item):
        log_level, painted = carried
        block_rows, block_mask = block_item
        off_x = pix_x[None, :] - block_rows[0][:, None]
        off_y = pix_y[None, :] - block_rows[1][:, None]
        exponent = (
            -0.5 * (block_rows[2][:, None] * off_x * off_x + block_rows[4][:, None] * off_y * off_y)
            - block_rows[3][:, None] * off_x * off_y
        )
        alpha_px = (block_rows[5] * block_mask)[:, None] * jnp.exp(exponent)
        fade_log = jnp.log1p(-alpha_px)
        running = jnp.cumsum(fade_log, axis=0)
        weights = alpha_px * jnp.exp(log_level[None, :] + running - fade_log)
        painted = painted + jnp.dot(block_rows[6:9], weights, precision=lax.Precision.HIGHEST)
        return ((log_level + running[-1], painted), None)

    initial = (jnp.zeros(pix_x.shape, jnp.float32), jnp.zeros((3, pix_x.shape[0]), jnp.float32))
    (log_level, painted), unused = lax.scan(block_step, initial, (grouped, block_masks))
    return painted


def body(
    params,
    adam_m,
    adam_v,
    cameras,
    exposure,
    entry_owner,
    entry_local,
    block_counts,
    tile_view,
    tile_spot,
    d_image,
):
    devices = lax.axis_size(("tiles", "gauss"))
    gauss_dev = params.shape[1]
    tile_dev, slot_count = entry_owner.shape
    entries = tile_dev * slot_count
    capacity = 3 * entries // (2 * devices)
    owners = entry_owner.reshape(entries)
    request = jnp.repeat(tile_view, slot_count) * gauss_dev + entry_local.reshape(entries)
    sort_order = jnp.argsort(owners, stable=True)
    sorted_owner = owners[sort_order]
    starts = jnp.searchsorted(sorted_owner, jnp.arange(devices, dtype=jnp.int32), side="left")
    ranked = jnp.arange(entries, dtype=jnp.int32) - starts[sorted_owner]
    target = jnp.zeros((entries,), jnp.int32).at[sort_order].set(sorted_owner * capacity + ranked)
    outgoing = jnp.full((devices * capacity,), -1, jnp.int32).at[target].set(request)
    incoming = lax.all_to_all(outgoing, ("tiles", "gauss"), split_axis=0, concat_axis=0, tiled=True)
    present = incoming >= 0
    across = IMG_W // TILE
    pixel_ids = jnp.arange(TPIX, dtype=jnp.int32)
    pix_x = ((tile_spot % across)[:, None] * TILE + pixel_ids[None, :] % TILE).astype(
        jnp.float32
    ) + 0.5
    pix_y = ((tile_spot // across)[:, None] * TILE + pixel_ids[None, :] // TILE).astype(
        jnp.float32
    ) + 0.5
    live_mask = (
        (jnp.arange(slot_count, dtype=jnp.int32) // BLOCK)[None, :] < block_counts[:, None]
    ).astype(jnp.float32)
    picker = (tile_view[:, None] == jnp.arange(VIEWS, dtype=jnp.int32)[None, :]).astype(jnp.float32)
    tile_gains = jnp.dot(picker, exposure, precision=lax.Precision.HIGHEST)
    tile_cameras = jnp.dot(picker, cameras, precision=lax.Precision.HIGHEST)
    replies = jnp.take(params, jnp.maximum(incoming, 0) % gauss_dev, axis=1)
    arrived = lax.all_to_all(replies, ("tiles", "gauss"), split_axis=1, concat_axis=1, tiled=True)
    entry_rows = (
        jnp.take(arrived, target, axis=1).reshape(PARAMS, tile_dev, slot_count).transpose(1, 0, 2)
    )

    def tile_grad(tile_item):
        row_block, camera_row, mask_row, x_row, y_row, gain_vec, cotangent = tile_item

        def tile_image(rows_in, gains_in):
            return gains_in[:, None] * render_blocks(
                project(rows_in, camera_row[:, None]), mask_row, x_row, y_row
            )

        rendered, pullback = jax.vjp(tile_image, row_block, gain_vec)
        return pullback(cotangent)

    grad_rows, grad_gains = lax.map(
        tile_grad, (entry_rows, tile_cameras, live_mask, pix_x, pix_y, tile_gains, d_image)
    )
    entry_grads = grad_rows.transpose(1, 0, 2).reshape(PARAMS, entries)
    outgoing_grads = (
        jnp.zeros((PARAMS, devices * capacity), jnp.float32).at[:, target].set(entry_grads)
    )
    returned = lax.all_to_all(
        outgoing_grads, ("tiles", "gauss"), split_axis=1, concat_axis=1, tiled=True
    )
    local_index = jnp.where(present, incoming % gauss_dev, gauss_dev)
    gradient = (
        jnp.zeros((PARAMS, gauss_dev + 1), jnp.float32).at[:, local_index].add(returned)[:, :-1]
    )
    expo_local = jnp.dot(picker.T, grad_gains, precision=lax.Precision.HIGHEST)
    exposure_grad = lax.psum(expo_local, ("tiles", "gauss")) / devices
    new_m = beta_first * adam_m + (1.0 - beta_first) * gradient
    new_v = beta_second * adam_v + (1.0 - beta_second) * gradient * gradient
    new_params = params - learn_rate * (new_m / fix_first) / (
        jnp.sqrt(new_v / fix_second) + adam_eps
    )
    return (new_params, new_m, new_v, exposure_grad)


def solution(mesh):
    placed = (
        P(None, ("tiles", "gauss")),
        P(None, ("tiles", "gauss")),
        P(None, ("tiles", "gauss")),
        P(),
        P(),
        P(("tiles", "gauss"), None),
        P(("tiles", "gauss"), None),
        P(("tiles", "gauss")),
        P(("tiles", "gauss")),
        P(("tiles", "gauss")),
        P(("tiles", "gauss"), None, None),
    )
    return jax.shard_map(
        body,
        mesh=mesh,
        in_specs=placed,
        out_specs=(
            P(None, ("tiles", "gauss")),
            P(None, ("tiles", "gauss")),
            P(None, ("tiles", "gauss")),
            P(),
        ),
        check_vma=False,
    )
```

profile of v0, /device:TPU:1, one launch (start us, length us, event | category | flops | bytes accessed | tf_op | source)
XLA Modules:
  0.0 854.1 jit_solution(9691868540588589673)
XLA Ops:
  7.2 23.0 %gather_fusion.1 = s32[4096]{0:T(1024)S(1)} fusion(s32[4096]{0:T(1024)S(1)} %bitcast.1032, s32[4096]{0:T(1024)S(1)} %get-tuple-element.1639), kind=kCustom, calls=%fused_computation.1 | custom fusion | bytes 49152 | tf_op jit(solution)/shard_map/gather | solution.py:221
  30.2 15.8 %while.148 = (s32[]{:T(128)}, u32[128]{0:T(128)S(1)}, u32[128]{0:T(128)S(1)}, s32[4096]{0:T(1024)S(1)}, s32[]{:T(128)}, /*index=5*/s32[]{:T(128)}, s32[]{}) while((s32[]{:T(128)}, u32[128]{0:T(128)S(1)}, u32[128]{0:T(128)S(1)}, s32[4096]{0:T(1024)S(1)}, s32[]{:T(128)}, /*index=5*/s32[]{:T(128)}, s32[]{}) %tuple.508), condition=%wide.region_2.3_spmd.clone, body=%wide.region_1.2_spmd.clone.sunk | while | flops 2692 | bytes 10340 | solution.py:222
  46.1 24.7 %gather_fusion.2 = s32[4096]{0:T(1024)S(1)} fusion(s32[128]{0:T(128)S(1)} %convert_element_type.20, s32[4096]{0:T(1024)S(1)} %broadcast_clamp_fusion.2), kind=kCustom, calls=%fused_computation.2 | custom fusion | bytes 49152 | tf_op jit(solution)/shard_map/gather | solution.py:223
  70.8 15.5 %scatter_custom_fusion = s32[4096]{0:T(1024)S(1)} fusion(s32[4096]{0:T(1024)S(1)} %get-tuple-element.1640, s32[4096]{0:T(1024)S(1)} %subtract_add_fusion, s32[]{:T(128)} %constant.484.clone.1), kind=kCustom, calls=%fused_computation.596 | custom fusion | bytes 16388 | tf_op jit(solution)/shard_map/scatter | solution.py:224
  86.5 15.5 %scatter_custom_fusion.1 = s32[6144]{0:T(1024)S(1)} fusion(s32[4096]{0:T(1024)S(1)} %get-tuple-element.1638, s32[4096]{0:T(1024)S(1)} %bitcast.1134, s32[]{:T(128)} %constant.483.clone.1), kind=kCustom, calls=%fused_computation.588 | custom fusion | bytes 24580 | tf_op jit(solution)/shard_map/scatter | solution.py:225
  102.8 11.5 %all-to-all-start = ((s32[128,48,1]{1,2,0:T(1,128)}), s32[128,48,1]{1,2,0:T(1,128)S(1)}, u32[]{:S(2)}, u32[]{:S(2)}) async-start(s32[128,48,1]{1,2,0:T(1,128)} %bitcast.81), calls=%async_computation | async-start | bytes 131072 | tf_op jit(solution)/shard_map/all_to_all | solution.py:226
  114.3 7.0 copy.134
  125.3 24.5 %gather_fusion.3 = f32[6144,59]{1,0:T(8,128)} fusion(f32[59,16384]{0,1:T(8,128)} %copy.134, s32[6144]{0:T(1024)S(1)} %broadcast_clamp_fusion), kind=kCustom, calls=%fused_computation.3 | custom fusion | bytes 2924544 | tf_op jit(solution)/shard_map/jit(_take)/gather | solution.py:242
  158.5 19.7 %all-to-all-start.1 = ((f32[128,1,2832]{2,1,0:T(1,128)}), f32[128,1,2832]{2,1,0:T(1,128)S(1)}, u32[]{:S(2)}, u32[]{:S(2)}) async-start(f32[128,1,2832]{2,1,0:T(1,128)} %reshape.9949), calls=%async_computation.1 | async-start | bytes 3014656 | tf_op jit(solution)/shard_map/all_to_all | solution.py:243
  178.7 23.3 %all-to-all-done.1 = f32[128,1,2832]{2,1,0:T(1,128)S(1)} async-done(((f32[128,1,2832]{2,1,0:T(1,128)}), f32[128,1,2832]{2,1,0:T(1,128)S(1)}, u32[]{:S(2)}, u32[]{:S(2)}) %all-to-all-start.1) | async-done | bytes 1450016 | tf_op jit(solution)/shard_map/all_to_all | solution.py:243
  212.1 14.2 %gather_fusion.4 = f32[4096,59]{1,0:T(8,128)} fusion(f32[59,6144]{0,1:T(8,128)S(1)} %bitcast.1042, s32[4096]{0:T(1024)S(1)} %get-tuple-element.1637), kind=kCustom, calls=%fused_computation.4 | custom fusion | bytes 1949696 | tf_op jit(solution)/shard_map/jit(_take)/gather | solution.py:245
  229.6 451.8 %while.147 = (s32[]{:T(128)}, f32[4,59,1024]{2,1,0:T(8,128)}, f32[4,3]{1,0:T(4,128)S(1)}, f32[4,59,1024]{2,1,0:T(8,128)}, f32[4,13]{1,0:T(4,128)S(1)}, /*index=5...) while((s32[]{:T(128)}, f32[4,59,1024]{2,1,0:T(8,128)}, ...), condition=%wide.region_37.38_spmd, body=%wide.region_5.37_spmd.sunk | while | flops 33596216 | bytes 15937833 | solution.py:259
  244.2 9.8 %fusion.236 = (f32[1024]{0:T(1024)S(1)}, f32[1,1,1024]{2,1,0:T(1,128)S(1)}, f32[1024]{0:T(1024)S(1)}, f32[1,1,1024]{2,1,0:T(1,128)S(1)}, f32[1,1,1024]{2,1,0:T(1...) fusion(f32[]{:T(128)} %broadcast.13728, f32[]{:T(128)} %bitcast.945, ...), kind=kLoop, calls=%fused_computation.632.clone.1 | loop fusion | flops 21504 | bytes 41028 | tf_op jit(solution)/shard_map/while/body/eval_jaxpr/jvp()/mul | solution.py:82
  265.0 20.0 %while.149 = (s32[]{:T(128)}, f32[256]{0:T(256)S(1)}, f32[3,256]{1,0:T(4,128)S(1)}, f32[4,256,256]{2,1,0:T(8,128)}, f32[4,256,1]{1,2,0:T(1,128)S(1)}, /*index=5*...) while((s32[]{:T(128)}, f32[256]{0:T(256)S(1)}, ...), condition=%wide.region_9.9_spmd.clone, body=%wide.region_6.8_spmd.clone.sunk | while | flops 14749193 | bytes 4594060 | solution.py:196
  285.9 32.6 %while.150 = (s32[]{:T(128)}, f32[256]{0:T(256)S(1)}, f32[4,9,256]{2,1,0:T(8,128)S(1)}, f32[4,256,256]{2,1,0:T(8,128)}, f32[4,3,256]{2,1,0:T(4,128)S(1)}, /*inde...) while((s32[]{:T(128)}, f32[256]{0:T(256)S(1)}, ...), condition=%wide.region_20.20_spmd.clone, body=%wide.region_10.19_spmd.clone.sunk | while | flops 15546372 | bytes 6922508 | solution.py:196
  318.8 7.5 negate_add_fusion.2
  357.2 9.8 %fusion.236 = (f32[1024]{0:T(1024)S(1)}, f32[1,1,1024]{2,1,0:T(1,128)S(1)}, f32[1024]{0:T(1024)S(1)}, f32[1,1,1024]{2,1,0:T(1,128)S(1)}, f32[1,1,1024]{2,1,0:T(1...) fusion(f32[]{:T(128)} %broadcast.13728, f32[]{:T(128)} %bitcast.945, ...), kind=kLoop, calls=%fused_computation.632.clone.1 | loop fusion | flops 21504 | bytes 41028 | tf_op jit(solution)/shard_map/while/body/eval_jaxpr/jvp()/mul | solution.py:82
  378.1 20.0 %while.149 = (s32[]{:T(128)}, f32[256]{0:T(256)S(1)}, f32[3,256]{1,0:T(4,128)S(1)}, f32[4,256,256]{2,1,0:T(8,128)}, f32[4,256,1]{1,2,0:T(1,128)S(1)}, /*index=5*...) while((s32[]{:T(128)}, f32[256]{0:T(256)S(1)}, ...), condition=%wide.region_9.9_spmd.clone, body=%wide.region_6.8_spmd.clone.sunk | while | flops 14749193 | bytes 4594060 | solution.py:196
  398.9 32.6 %while.150 = (s32[]{:T(128)}, f32[256]{0:T(256)S(1)}, f32[4,9,256]{2,1,0:T(8,128)S(1)}, f32[4,256,256]{2,1,0:T(8,128)}, f32[4,3,256]{2,1,0:T(4,128)S(1)}, /*inde...) while((s32[]{:T(128)}, f32[256]{0:T(256)S(1)}, ...), condition=%wide.region_20.20_spmd.clone, body=%wide.region_10.19_spmd.clone.sunk | while | flops 15546372 | bytes 6922508 | solution.py:196
  431.9 7.5 negate_add_fusion.2
  470.2 9.8 %fusion.236 = (f32[1024]{0:T(1024)S(1)}, f32[1,1,1024]{2,1,0:T(1,128)S(1)}, f32[1024]{0:T(1024)S(1)}, f32[1,1,1024]{2,1,0:T(1,128)S(1)}, f32[1,1,1024]{2,1,0:T(1...) fusion(f32[]{:T(128)} %broadcast.13728, f32[]{:T(128)} %bitcast.945, ...), kind=kLoop, calls=%fused_computation.632.clone.1 | loop fusion | flops 21504 | bytes 41028 | tf_op jit(solution)/shard_map/while/body/eval_jaxpr/jvp()/mul | solution.py:82
  491.0 20.0 %while.149 = (s32[]{:T(128)}, f32[256]{0:T(256)S(1)}, f32[3,256]{1,0:T(4,128)S(1)}, f32[4,256,256]{2,1,0:T(8,128)}, f32[4,256,1]{1,2,0:T(1,128)S(1)}, /*index=5*...) while((s32[]{:T(128)}, f32[256]{0:T(256)S(1)}, ...), condition=%wide.region_9.9_spmd.clone, body=%wide.region_6.8_spmd.clone.sunk | while | flops 14749193 | bytes 4594060 | solution.py:196
  511.8 32.6 %while.150 = (s32[]{:T(128)}, f32[256]{0:T(256)S(1)}, f32[4,9,256]{2,1,0:T(8,128)S(1)}, f32[4,256,256]{2,1,0:T(8,128)}, f32[4,3,256]{2,1,0:T(4,128)S(1)}, /*inde...) while((s32[]{:T(128)}, f32[256]{0:T(256)S(1)}, ...), condition=%wide.region_20.20_spmd.clone, body=%wide.region_10.19_spmd.clone.sunk | while | flops 15546372 | bytes 6922508 | solution.py:196
  544.8 7.5 negate_add_fusion.2
  583.1 9.8 %fusion.236 = (f32[1024]{0:T(1024)S(1)}, f32[1,1,1024]{2,1,0:T(1,128)S(1)}, f32[1024]{0:T(1024)S(1)}, f32[1,1,1024]{2,1,0:T(1,128)S(1)}, f32[1,1,1024]{2,1,0:T(1...) fusion(f32[]{:T(128)} %broadcast.13728, f32[]{:T(128)} %bitcast.945, ...), kind=kLoop, calls=%fused_computation.632.clone.1 | loop fusion | flops 21504 | bytes 41028 | tf_op jit(solution)/shard_map/while/body/eval_jaxpr/jvp()/mul | solution.py:82
  603.9 20.0 %while.149 = (s32[]{:T(128)}, f32[256]{0:T(256)S(1)}, f32[3,256]{1,0:T(4,128)S(1)}, f32[4,256,256]{2,1,0:T(8,128)}, f32[4,256,1]{1,2,0:T(1,128)S(1)}, /*index=5*...) while((s32[]{:T(128)}, f32[256]{0:T(256)S(1)}, ...), condition=%wide.region_9.9_spmd.clone, body=%wide.region_6.8_spmd.clone.sunk | while | flops 14749193 | bytes 4594060 | solution.py:196
  624.8 32.6 %while.150 = (s32[]{:T(128)}, f32[256]{0:T(256)S(1)}, f32[4,9,256]{2,1,0:T(8,128)S(1)}, f32[4,256,256]{2,1,0:T(8,128)}, f32[4,3,256]{2,1,0:T(4,128)S(1)}, /*inde...) while((s32[]{:T(128)}, f32[256]{0:T(256)S(1)}, ...), condition=%wide.region_20.20_spmd.clone, body=%wide.region_10.19_spmd.clone.sunk | while | flops 15546372 | bytes 6922508 | solution.py:196
  657.7 7.5 negate_add_fusion.2
  686.1 11.9 %scatter_custom_fusion.2 = f32[59,6144]{0,1:T(8,128)S(1)} fusion(s32[4096]{0:T(1024)S(1)} %get-tuple-element.1638, f32[4096,59]{1,0:T(8,128)} %copy.139, f32[]{:T(128)} %constant.482.clone.1), kind=kCustom, calls=%fused_computation.563 | custom fusion | bytes 1450496 | tf_op jit(solution)/shard_map/scatter | solution.py:264
  708.3 75.3 %psum.7 = f32[4,3]{0,1:T(4,128)S(1)} all-reduce(f32[4,3]{0,1:T(4,128)S(1)} %fusion.171), channel_id=1, replica_groups=mesh['tiles'=16,'gauss'=8] {'tiles','gauss'}, use_global_device_ids=true, to_apply=%region_40.41 | all-reduce | flops 12 | bytes 96 | tf_op jit(solution)/shard_map/psum | solution.py:274
  792.1 37.6 %scatter_custom_fusion.3 = f32[59,16385]{0,1:T(8,128)} fusion(s32[6144]{0:T(1024)S(1)} %bitcast.1132, f32[6144,59]{1,0:T(8,128)} %bitcast.1081, f32[]{:T(128)} %constant.482.clone.1), kind=kCustom, calls=%fused_computation.557 | custom fusion | flops 362496 | bytes 3867372 | tf_op jit(solution)/shard_map/scatter-add | solution.py:271
  842.2 11.6 %divide_subtract_fusion = (f32[59,16384]{1,0:T(8,128)}, f32[59,16384]{1,0:T(8,128)}, f32[59,16384]{1,0:T(8,128)}) fusion(f32[59,16384]{1,0:T(8,128)} %param.19, f32[59,16384]{1,0:T(8,128)} %copy.145, f32[59,16384]{1,0:T(8,128)} %param.20, f32[59,16384]{1,0:T(8,128)} %param.21), kind=kLoop, calls=%fused_computation.560 | loop fusion | flops 11599872 | bytes 27066368 | tf_op jit(solution)/shard_map/sub | solution.py:277
  (1205 shorter events, 417.8 us)
Async XLA Ops:
  0.6 177.8 %copy-start = (f32[4,13]{1,0:T(4,128)S(1)}, f32[4,13]{1,0:T(4,128)}, u32[]{:S(2)}) copy-start(f32[4,13]{1,0:T(4,128)} %param.22) | copy-start | bytes 628
  46.1 40.3 %copy-start.6 = (s32[4]{0:T(128)S(1)}, s32[4]{0:T(128)}, u32[]{:S(2)}) copy-start(s32[4]{0:T(128)} %param.27) | copy-start | bytes 52
  46.1 40.3 %copy-start.2 = (s32[4,1024]{1,0:T(4,128)S(1)}, s32[4,1024]{1,0:T(4,128)}, u32[]{:S(2)}) copy-start(s32[4,1024]{1,0:T(4,128)} %param.25) | copy-start | bytes 49156
  102.8 20.8 %all-to-all-start = ((s32[128,48,1]{1,2,0:T(1,128)}), s32[128,48,1]{1,2,0:T(1,128)S(1)}, u32[]{:S(2)}, u32[]{:S(2)}) async-start(s32[128,48,1]{1,2,0:T(1,128)} %bitcast.81), calls=%async_computation | async-start | bytes 131072 | tf_op jit(solution)/shard_map/all_to_all | solution.py:226
  153.0 25.2 %copy-start.5 = (s32[4]{0:T(128)S(1)}, s32[4]{0:T(128)}, u32[]{:S(2)}) copy-start(s32[4]{0:T(128)} %param.28) | copy-start | bytes 52
  153.0 25.2 %copy-start.4 = (f32[4,3]{1,0:T(4,128)S(1)}, f32[4,3]{1,0:T(4,128)}, u32[]{:S(2)}) copy-start(f32[4,3]{1,0:T(4,128)} %param.23) | copy-start | bytes 148
  153.0 25.7 %copy-start.3 = (s32[4]{0:T(128)S(1)}, s32[4]{0:T(128)}, u32[]{:S(2)}) copy-start(s32[4]{0:T(128)} %param.26) | copy-start | bytes 52
  158.5 43.6 %all-to-all-start.1 = ((f32[128,1,2832]{2,1,0:T(1,128)}), f32[128,1,2832]{2,1,0:T(1,128)S(1)}, u32[]{:S(2)}, u32[]{:S(2)}) async-start(f32[128,1,2832]{2,1,0:T(1,128)} %reshape.9949), calls=%async_computation.1 | async-start | bytes 3014656 | tf_op jit(solution)/shard_map/all_to_all | solution.py:243
  703.4 80.8 %all-to-all-start.2 = ((f32[128,1,2832]{2,1,0:T(1,128)}), f32[128,1,2832]{2,1,0:T(1,128)S(1)}, u32[]{:S(2)}, u32[]{:S(2)}) async-start(f32[128,1,2832]{2,1,0:T(1,128)} %reshape.9951), calls=%async_computation.2 | async-start | bytes 3014656 | tf_op jit(solution)/shard_map/all_to_all | solution.py:266
  842.2 11.6 %copy-start.1 = (f32[4,13]{1,0:T(4,128)S(1)}, f32[4,13]{1,0:T(4,128)}, u32[]{:S(2)}) copy-start(f32[4,13]{1,0:T(4,128)} %param.22) | copy-start | bytes 628
where the time goes:
time: 870 us; the launch traced here: 854 us
  other arithmetic  399 us (46%)
  local copies, waits for them, and re-layouts  215 us (25%)
  blocking collectives  75.3 us (9%)
  matrix products  51.3 us (6%)
  loops' own time  51 us (6%)
  starting transfers between devices  35.8 us (4%)
  waiting for transfers between devices  25.6 us (3%)
    psum x1, blocking collectives, body(): exposure_grad = lax.psum(expo_local, ('tiles', 'gauss')) / devices  75.3 us
    another operation x157, other arithmetic  53.4 us
    dot_general x48, matrix products, block_step(): jnp.dot(block_rows[6:9], weights, precision=lax.Precision.HIGHEST)  50.7 us
    another operation x1, loops' own time, body(): lax.map(tile_grad, (entry_rows, tile_cameras, live_mask, pix_x, pix_y, ti...  47.4 us
    dynamic_update_slice x64, other arithmetic, render_blocks(): lax.scan(block_step, initial, (grouped, block_masks))  43.3 us
    mul x4, other arithmetic, project(): screen_y = focal_len * viewed[1] * inverse_depth + 0.5 * IMG_H  39 us
    scatter-add x1, other arithmetic, body(): jnp.zeros((PARAMS, gauss_dev + 1), jnp.float32).at[:, local_index]  37.6 us
    mul x16, other arithmetic, project(): (jac_w[row_at][0] * rotation[0][col_at] + jac_w[row_at][1] * rotation[1][...  35.4 us
  transfers between devices with their start and end apart: 3, of which 2 were waited for; matrix products, arithmetic and copies ran while one was open for 1% of the time, Pallas kernels for 0%

commit v1 on v0

--- a/solution.py
+++ b/solution.py
@@ -271,7 +271,7 @@
         jnp.zeros((PARAMS, gauss_dev + 1), jnp.float32).at[:, local_index].add(returned)[:, :-1]
     )
     expo_local = jnp.dot(picker.T, grad_gains, precision=lax.Precision.HIGHEST)
-    exposure_grad = lax.psum(expo_local, ("tiles", "gauss")) / devices
+    exposure_grad = jnp.sum(lax.all_gather(expo_local, ("tiles", "gauss")), axis=0) / devices
     new_m = beta_first * adam_m + (1.0 - beta_first) * gradient
     new_v = beta_second * adam_v + (1.0 - beta_second) * gradient * gradient
     new_params = params - learn_rate * (new_m / fix_first) / (

time: 870 us -> 843 us (0.969)
  blocking collectives: 75.3 us -> 48.7 us
    psum x1 -> x0, blocking collectives: 75.3 us -> none  [body(): exposure_grad = lax.psum(expo_local, ('tiles', 'gauss')) / devices]
    all_gather x0 -> x1, blocking collectives: none -> 48.7 us  [body(): lax.all_gather(expo_local, ('tiles', 'gauss'))]
    unnamed x25 -> x24, local copies, waits for them, and re-layouts: 34.2 us -> 33.7 us
where the time goes in v1:
time: 843 us; the launch traced here: 828 us
  other arithmetic  400 us (47%)
  local copies, waits for them, and re-layouts  214 us (25%)
  matrix products  51.4 us (6%)
  loops' own time  51 us (6%)
  blocking collectives  48.7 us (6%)
  starting transfers between devices  35.8 us (4%)
  waiting for transfers between devices  25.6 us (3%)
    another operation x157, other arithmetic  53.4 us
    dot_general x48, matrix products, block_step(): jnp.dot(block_rows[6:9], weights, precision=lax.Precision.HIGHEST)  50.7 us
    all_gather x1, blocking collectives, body(): lax.all_gather(expo_local, ('tiles', 'gauss'))  48.7 us
    another operation x1, loops' own time, body(): lax.map(tile_grad, (entry_rows, tile_cameras, live_mask, pix_x, pix_y, ti...  47.4 us
    dynamic_update_slice x64, other arithmetic, render_blocks(): lax.scan(block_step, initial, (grouped, block_masks))  43.3 us
    mul x4, other arithmetic, project(): screen_y = focal_len * viewed[1] * inverse_depth + 0.5 * IMG_H  39 us
    scatter-add x1, other arithmetic, body(): jnp.zeros((PARAMS, gauss_dev + 1), jnp.float32).at[:, local_index]  37.6 us
    mul x16, other arithmetic, project(): (jac_w[row_at][0] * rotation[0][col_at] + jac_w[row_at][1] * rotation[1][...  35.4 us
  transfers between devices with their start and end apart: 3, of which 2 were waited for; matrix products, arithmetic and copies ran while one was open for 1% of the time, Pallas kernels for 0%

profile of v1, /device:TPU:1, one launch (start us, length us, event | category | flops | bytes accessed | tf_op | source)
XLA Modules:
  0.0 828.0 jit_solution(4833168119230224413)
XLA Ops:
  7.2 23.0 %gather_fusion.1 = s32[4096]{0:T(1024)S(1)} fusion(s32[4096]{0:T(1024)S(1)} %bitcast.1034, s32[4096]{0:T(1024)S(1)} %get-tuple-element.1635), kind=kCustom, calls=%fused_computation.1 | custom fusion | bytes 49152 | tf_op jit(solution)/shard_map/gather | solution.py:221
  30.2 15.8 %while.148 = (s32[]{:T(128)}, u32[128]{0:T(128)S(1)}, u32[128]{0:T(128)S(1)}, s32[4096]{0:T(1024)S(1)}, s32[]{:T(128)}, /*index=5*/s32[]{:T(128)}, s32[]{}) while((s32[]{:T(128)}, u32[128]{0:T(128)S(1)}, u32[128]{0:T(128)S(1)}, s32[4096]{0:T(1024)S(1)}, s32[]{:T(128)}, /*index=5*/s32[]{:T(128)}, s32[]{}) %tuple.507), condition=%wide.region_2.3_spmd.clone, body=%wide.region_1.2_spmd.clone.sunk | while | flops 2692 | bytes 10340 | solution.py:222
  46.1 24.7 %gather_fusion.2 = s32[4096]{0:T(1024)S(1)} fusion(s32[128]{0:T(128)S(1)} %convert_element_type.20, s32[4096]{0:T(1024)S(1)} %broadcast_clamp_fusion.2), kind=kCustom, calls=%fused_computation.2 | custom fusion | bytes 49152 | tf_op jit(solution)/shard_map/gather | solution.py:223
  70.8 15.5 %scatter_custom_fusion = s32[4096]{0:T(1024)S(1)} fusion(s32[4096]{0:T(1024)S(1)} %get-tuple-element.1636, s32[4096]{0:T(1024)S(1)} %subtract_add_fusion, s32[]{:T(128)} %constant.485.clone.1), kind=kCustom, calls=%fused_computation.597 | custom fusion | bytes 16388 | tf_op jit(solution)/shard_map/scatter | solution.py:224
  86.5 15.5 %scatter_custom_fusion.1 = s32[6144]{0:T(1024)S(1)} fusion(s32[4096]{0:T(1024)S(1)} %get-tuple-element.1634, s32[4096]{0:T(1024)S(1)} %bitcast.1136, s32[]{:T(128)} %constant.484.clone.1), kind=kCustom, calls=%fused_computation.589 | custom fusion | bytes 24580 | tf_op jit(solution)/shard_map/scatter | solution.py:225
  102.8 11.5 %all-to-all-start = ((s32[128,48,1]{1,2,0:T(1,128)}), s32[128,48,1]{1,2,0:T(1,128)S(1)}, u32[]{:S(2)}, u32[]{:S(2)}) async-start(s32[128,48,1]{1,2,0:T(1,128)} %bitcast.81), calls=%async_computation | async-start | bytes 131072 | tf_op jit(solution)/shard_map/all_to_all | solution.py:226
  114.3 7.0 copy.134
  125.3 24.5 %gather_fusion.3 = f32[6144,59]{1,0:T(8,128)} fusion(f32[59,16384]{0,1:T(8,128)} %copy.134, s32[6144]{0:T(1024)S(1)} %broadcast_clamp_fusion), kind=kCustom, calls=%fused_computation.3 | custom fusion | bytes 2924544 | tf_op jit(solution)/shard_map/jit(_take)/gather | solution.py:242
  158.5 19.7 %all-to-all-start.1 = ((f32[128,1,2832]{2,1,0:T(1,128)}), f32[128,1,2832]{2,1,0:T(1,128)S(1)}, u32[]{:S(2)}, u32[]{:S(2)}) async-start(f32[128,1,2832]{2,1,0:T(1,128)} %reshape.9953), calls=%async_computation.1 | async-start | bytes 3014656 | tf_op jit(solution)/shard_map/all_to_all | solution.py:243
  178.7 23.3 %all-to-all-done.1 = f32[128,1,2832]{2,1,0:T(1,128)S(1)} async-done(((f32[128,1,2832]{2,1,0:T(1,128)}), f32[128,1,2832]{2,1,0:T(1,128)S(1)}, u32[]{:S(2)}, u32[]{:S(2)}) %all-to-all-start.1) | async-done | bytes 1450016 | tf_op jit(solution)/shard_map/all_to_all | solution.py:243
  212.1 14.2 %gather_fusion.4 = f32[4096,59]{1,0:T(8,128)} fusion(f32[59,6144]{0,1:T(8,128)S(1)} %bitcast.1044, s32[4096]{0:T(1024)S(1)} %get-tuple-element.1633), kind=kCustom, calls=%fused_computation.4 | custom fusion | bytes 1949696 | tf_op jit(solution)/shard_map/jit(_take)/gather | solution.py:245
  229.6 451.8 %while.147 = (s32[]{:T(128)}, f32[4,59,1024]{2,1,0:T(8,128)}, f32[4,3]{1,0:T(4,128)S(1)}, f32[4,59,1024]{2,1,0:T(8,128)}, f32[4,13]{1,0:T(4,128)S(1)}, /*index=5...) while((s32[]{:T(128)}, f32[4,59,1024]{2,1,0:T(8,128)}, ...), condition=%wide.region_37.38_spmd, body=%wide.region_5.37_spmd.sunk | while | flops 33596216 | bytes 15937833 | solution.py:259
  244.2 9.8 %fusion.235 = (f32[1024]{0:T(1024)S(1)}, f32[1,1,1024]{2,1,0:T(1,128)S(1)}, f32[1024]{0:T(1024)S(1)}, f32[1,1,1024]{2,1,0:T(1,128)S(1)}, f32[1,1,1024]{2,1,0:T(1...) fusion(f32[]{:T(128)} %broadcast.13728, f32[]{:T(128)} %bitcast.947, ...), kind=kLoop, calls=%fused_computation.632.clone.1 | loop fusion | flops 21504 | bytes 41028 | tf_op jit(solution)/shard_map/while/body/eval_jaxpr/jvp()/mul | solution.py:82
  265.0 20.0 %while.149 = (s32[]{:T(128)}, f32[256]{0:T(256)S(1)}, f32[3,256]{1,0:T(4,128)S(1)}, f32[4,256,256]{2,1,0:T(8,128)}, f32[4,256,1]{1,2,0:T(1,128)S(1)}, /*index=5*...) while((s32[]{:T(128)}, f32[256]{0:T(256)S(1)}, ...), condition=%wide.region_9.9_spmd.clone, body=%wide.region_6.8_spmd.clone.sunk | while | flops 14749193 | bytes 4594060 | solution.py:196
  285.9 32.6 %while.150 = (s32[]{:T(128)}, f32[256]{0:T(256)S(1)}, f32[4,9,256]{2,1,0:T(8,128)S(1)}, f32[4,256,256]{2,1,0:T(8,128)}, f32[4,3,256]{2,1,0:T(4,128)S(1)}, /*inde...) while((s32[]{:T(128)}, f32[256]{0:T(256)S(1)}, ...), condition=%wide.region_20.20_spmd.clone, body=%wide.region_10.19_spmd.clone.sunk | while | flops 15546372 | bytes 6922508 | solution.py:196
  318.8 7.5 negate_add_fusion.2
  357.2 9.8 %fusion.235 = (f32[1024]{0:T(1024)S(1)}, f32[1,1,1024]{2,1,0:T(1,128)S(1)}, f32[1024]{0:T(1024)S(1)}, f32[1,1,1024]{2,1,0:T(1,128)S(1)}, f32[1,1,1024]{2,1,0:T(1...) fusion(f32[]{:T(128)} %broadcast.13728, f32[]{:T(128)} %bitcast.947, ...), kind=kLoop, calls=%fused_computation.632.clone.1 | loop fusion | flops 21504 | bytes 41028 | tf_op jit(solution)/shard_map/while/body/eval_jaxpr/jvp()/mul | solution.py:82
  378.1 20.0 %while.149 = (s32[]{:T(128)}, f32[256]{0:T(256)S(1)}, f32[3,256]{1,0:T(4,128)S(1)}, f32[4,256,256]{2,1,0:T(8,128)}, f32[4,256,1]{1,2,0:T(1,128)S(1)}, /*index=5*...) while((s32[]{:T(128)}, f32[256]{0:T(256)S(1)}, ...), condition=%wide.region_9.9_spmd.clone, body=%wide.region_6.8_spmd.clone.sunk | while | flops 14749193 | bytes 4594060 | solution.py:196
  398.9 32.6 %while.150 = (s32[]{:T(128)}, f32[256]{0:T(256)S(1)}, f32[4,9,256]{2,1,0:T(8,128)S(1)}, f32[4,256,256]{2,1,0:T(8,128)}, f32[4,3,256]{2,1,0:T(4,128)S(1)}, /*inde...) while((s32[]{:T(128)}, f32[256]{0:T(256)S(1)}, ...), condition=%wide.region_20.20_spmd.clone, body=%wide.region_10.19_spmd.clone.sunk | while | flops 15546372 | bytes 6922508 | solution.py:196
  431.9 7.5 negate_add_fusion.2
  470.2 9.8 %fusion.235 = (f32[1024]{0:T(1024)S(1)}, f32[1,1,1024]{2,1,0:T(1,128)S(1)}, f32[1024]{0:T(1024)S(1)}, f32[1,1,1024]{2,1,0:T(1,128)S(1)}, f32[1,1,1024]{2,1,0:T(1...) fusion(f32[]{:T(128)} %broadcast.13728, f32[]{:T(128)} %bitcast.947, ...), kind=kLoop, calls=%fused_computation.632.clone.1 | loop fusion | flops 21504 | bytes 41028 | tf_op jit(solution)/shard_map/while/body/eval_jaxpr/jvp()/mul | solution.py:82
  491.0 20.0 %while.149 = (s32[]{:T(128)}, f32[256]{0:T(256)S(1)}, f32[3,256]{1,0:T(4,128)S(1)}, f32[4,256,256]{2,1,0:T(8,128)}, f32[4,256,1]{1,2,0:T(1,128)S(1)}, /*index=5*...) while((s32[]{:T(128)}, f32[256]{0:T(256)S(1)}, ...), condition=%wide.region_9.9_spmd.clone, body=%wide.region_6.8_spmd.clone.sunk | while | flops 14749193 | bytes 4594060 | solution.py:196
  511.8 32.6 %while.150 = (s32[]{:T(128)}, f32[256]{0:T(256)S(1)}, f32[4,9,256]{2,1,0:T(8,128)S(1)}, f32[4,256,256]{2,1,0:T(8,128)}, f32[4,3,256]{2,1,0:T(4,128)S(1)}, /*inde...) while((s32[]{:T(128)}, f32[256]{0:T(256)S(1)}, ...), condition=%wide.region_20.20_spmd.clone, body=%wide.region_10.19_spmd.clone.sunk | while | flops 15546372 | bytes 6922508 | solution.py:196
  544.8 7.5 negate_add_fusion.2
  583.1 9.8 %fusion.235 = (f32[1024]{0:T(1024)S(1)}, f32[1,1,1024]{2,1,0:T(1,128)S(1)}, f32[1024]{0:T(1024)S(1)}, f32[1,1,1024]{2,1,0:T(1,128)S(1)}, f32[1,1,1024]{2,1,0:T(1...) fusion(f32[]{:T(128)} %broadcast.13728, f32[]{:T(128)} %bitcast.947, ...), kind=kLoop, calls=%fused_computation.632.clone.1 | loop fusion | flops 21504 | bytes 41028 | tf_op jit(solution)/shard_map/while/body/eval_jaxpr/jvp()/mul | solution.py:82
  603.9 20.0 %while.149 = (s32[]{:T(128)}, f32[256]{0:T(256)S(1)}, f32[3,256]{1,0:T(4,128)S(1)}, f32[4,256,256]{2,1,0:T(8,128)}, f32[4,256,1]{1,2,0:T(1,128)S(1)}, /*index=5*...) while((s32[]{:T(128)}, f32[256]{0:T(256)S(1)}, ...), condition=%wide.region_9.9_spmd.clone, body=%wide.region_6.8_spmd.clone.sunk | while | flops 14749193 | bytes 4594060 | solution.py:196
  624.8 32.6 %while.150 = (s32[]{:T(128)}, f32[256]{0:T(256)S(1)}, f32[4,9,256]{2,1,0:T(8,128)S(1)}, f32[4,256,256]{2,1,0:T(8,128)}, f32[4,3,256]{2,1,0:T(4,128)S(1)}, /*inde...) while((s32[]{:T(128)}, f32[256]{0:T(256)S(1)}, ...), condition=%wide.region_20.20_spmd.clone, body=%wide.region_10.19_spmd.clone.sunk | while | flops 15546372 | bytes 6922508 | solution.py:196
  657.7 7.5 negate_add_fusion.2
  686.1 11.9 %scatter_custom_fusion.2 = f32[59,6144]{0,1:T(8,128)S(1)} fusion(s32[4096]{0:T(1024)S(1)} %get-tuple-element.1634, f32[4096,59]{1,0:T(8,128)} %copy.139, f32[]{:T(128)} %constant.483.clone.1), kind=kCustom, calls=%fused_computation.563 | custom fusion | bytes 1450496 | tf_op jit(solution)/shard_map/scatter | solution.py:264
  708.3 48.7 %all-gather.1 = f32[128,4,3]{2,1,0:T(4,128)S(1)} all-gather(f32[1,4,3]{2,1,0:T(4,128)S(1)} %convolution_bitcast_fusion.1), channel_id=2, replica_groups=mesh['tiles'=16,'gauss'=8] {'tiles','gauss'}, dimensions={0}, use_global_device_ids=true | all-gather | bytes 6192 | tf_op jit(solution)/shard_map/all_gather | solution.py:274
  765.9 37.6 %scatter_custom_fusion.3 = f32[59,16385]{0,1:T(8,128)} fusion(s32[6144]{0:T(1024)S(1)} %bitcast.1134, f32[6144,59]{1,0:T(8,128)} %bitcast.1083, f32[]{:T(128)} %constant.483.clone.1), kind=kCustom, calls=%fused_computation.557 | custom fusion | flops 362496 | bytes 3867372 | tf_op jit(solution)/shard_map/scatter-add | solution.py:271
  816.0 11.6 %divide_subtract_fusion = (f32[59,16384]{1,0:T(8,128)}, f32[59,16384]{1,0:T(8,128)}, f32[59,16384]{1,0:T(8,128)}) fusion(f32[59,16384]{1,0:T(8,128)} %param.19, f32[59,16384]{1,0:T(8,128)} %copy.146, f32[59,16384]{1,0:T(8,128)} %param.20, f32[59,16384]{1,0:T(8,128)} %param.21), kind=kLoop, calls=%fused_computation.560 | loop fusion | flops 11599872 | bytes 27066368 | tf_op jit(solution)/shard_map/sub | solution.py:277
  (1205 shorter events, 418.2 us)
Async XLA Ops:
  0.6 177.8 %copy-start = (f32[4,13]{1,0:T(4,128)S(1)}, f32[4,13]{1,0:T(4,128)}, u32[]{:S(2)}) copy-start(f32[4,13]{1,0:T(4,128)} %param.22) | copy-start | bytes 628
  46.1 40.3 %copy-start.6 = (s32[4]{0:T(128)S(1)}, s32[4]{0:T(128)}, u32[]{:S(2)}) copy-start(s32[4]{0:T(128)} %param.27) | copy-start | bytes 52
  46.1 40.3 %copy-start.2 = (s32[4,1024]{1,0:T(4,128)S(1)}, s32[4,1024]{1,0:T(4,128)}, u32[]{:S(2)}) copy-start(s32[4,1024]{1,0:T(4,128)} %param.25) | copy-start | bytes 49156
  102.8 20.8 %all-to-all-start = ((s32[128,48,1]{1,2,0:T(1,128)}), s32[128,48,1]{1,2,0:T(1,128)S(1)}, u32[]{:S(2)}, u32[]{:S(2)}) async-start(s32[128,48,1]{1,2,0:T(1,128)} %bitcast.81), calls=%async_computation | async-start | bytes 131072 | tf_op jit(solution)/shard_map/all_to_all | solution.py:226
  153.0 25.2 %copy-start.5 = (s32[4]{0:T(128)S(1)}, s32[4]{0:T(128)}, u32[]{:S(2)}) copy-start(s32[4]{0:T(128)} %param.28) | copy-start | bytes 52
  153.0 25.2 %copy-start.4 = (f32[4,3]{1,0:T(4,128)S(1)}, f32[4,3]{1,0:T(4,128)}, u32[]{:S(2)}) copy-start(f32[4,3]{1,0:T(4,128)} %param.23) | copy-start | bytes 148
  153.0 25.7 %copy-start.3 = (s32[4]{0:T(128)S(1)}, s32[4]{0:T(128)}, u32[]{:S(2)}) copy-start(s32[4]{0:T(128)} %param.26) | copy-start | bytes 52
  158.5 43.6 %all-to-all-start.1 = ((f32[128,1,2832]{2,1,0:T(1,128)}), f32[128,1,2832]{2,1,0:T(1,128)S(1)}, u32[]{:S(2)}, u32[]{:S(2)}) async-start(f32[128,1,2832]{2,1,0:T(1,128)} %reshape.9953), calls=%async_computation.1 | async-start | bytes 3014656 | tf_op jit(solution)/shard_map/all_to_all | solution.py:243
  703.4 54.4 %all-to-all-start.2 = ((f32[128,1,2832]{2,1,0:T(1,128)}), f32[128,1,2832]{2,1,0:T(1,128)S(1)}, u32[]{:S(2)}, u32[]{:S(2)}) async-start(f32[128,1,2832]{2,1,0:T(1,128)} %reshape.9955), calls=%async_computation.2 | async-start | bytes 3014656 | tf_op jit(solution)/shard_map/all_to_all | solution.py:266
  816.0 11.6 %copy-start.1 = (f32[4,13]{1,0:T(4,128)S(1)}, f32[4,13]{1,0:T(4,128)}, u32[]{:S(2)}) copy-start(f32[4,13]{1,0:T(4,128)} %param.22) | copy-start | bytes 628
